TPU v7x, 32 devices: a whole 2x2x4 slice. The times are simulated.
32 devices in a mesh: row: 8 (over y, x, core), col: 4 (over z).
Axes of the slice: x: 2, y: 2, z: 4, core: 2. Of those that a mesh axis runs over, the one named last changes fastest.
Arguments:
- base_weights: bfloat16 [2, 8192, 28672], P(None, 'row', 'col'), may hold values from -6 to 6
- left_factors: bfloat16 [2, 8192, 4, 128], P(None, 'row', 'col'), may hold values from -6 to 6
- right_factors: bfloat16 [2, 4, 128, 28672], P(None, 'col', None, 'row'), may hold values from -6 to 6
- client_adapter_ranks: int32 [4], replicated, may hold values from 16 to 128, as said below
- step_counts: int32 [4], replicated, may hold values from 100 to 1000
- worker_slot: int32 [4], replicated, may hold values from 0 to 3, each once
Outputs:
- merged: bfloat16 [2, 8192, 28672], P(None, 'row', 'col')
Inputs may be any that keep to these rules, and one draw needn't show every extreme that they name: `client_adapter_ranks`: each rank is a multiple of 16; the ranks sum to 256; at least one rank equals 128. `worker_slot`: a permutation: every slot holds exactly one worker's factors.
All inputs are finite; a program needn't handle non-finite values.
Results may differ from a plain program's by a relative error of at most 0.0045.
Values may be sent and summed in bfloat16 or wider, within the bound.
No kernel may reach another device: no remote copies, remote signals or barrier semaphores. Data moves between devices by JAX's collectives and lax.ppermute only.
A program may use at most 192 MiB of HBM per device.

v0:
```python
import jax
import jax.numpy as jnp
from jax import lax
from jax.sharding import PartitionSpec as P

ADAPTER_ALPHA = 32


def slot_tables(client_adapter_ranks, step_counts, worker_slot):
    workers = client_adapter_ranks.shape[0]
    slot_ids = jnp.arange(workers, dtype=jnp.int32)
    slot_hot = worker_slot[:, None] == slot_ids[None, :]
    rank_slot = jnp.sum(jnp.where(slot_hot, client_adapter_ranks[:, None], 0), axis=0)
    counts = step_counts.astype(jnp.float32)
    per_step_portion = counts / jnp.sum(counts)
    client_scale = ADAPTER_ALPHA * per_step_portion / client_adapter_ranks.astype(jnp.float32)
    slot_scale_factor = jnp.sum(jnp.where(slot_hot, client_scale[:, None], 0.0), axis=0)
    return (rank_slot, slot_scale_factor)


def merge_tile(base_tile, left_piece, right_piece):
    tile_rows = base_tile.shape[0]
    rank_cap = right_piece.shape[1]
    block_width = right_piece.shape[2]
    row_count = lax.axis_size("row")
    col_count = lax.axis_size("col")
    row_ratio = row_count // col_count
    left_all = lax.all_gather(left_piece, "col", axis=1, tiled=True)
    sub_width = block_width // row_count
    split_view = right_piece.reshape(1, rank_cap, row_count, sub_width)
    spread = lax.all_to_all(split_view, "row", split_axis=2, concat_axis=2, tiled=True)
    pair_view = spread.reshape(1, rank_cap, col_count, row_ratio, sub_width)
    slot_pieces = lax.all_to_all(pair_view, "col", split_axis=2, concat_axis=0, tiled=True)
    join_view = slot_pieces.reshape(col_count, rank_cap, row_ratio, 1, sub_width)
    joined = lax.all_gather(join_view, "row", axis=3, tiled=True)
    right_cols = joined.reshape(col_count, rank_cap, row_ratio * block_width)
    left_flat = left_all.reshape(tile_rows, -1)
    right_flat = right_cols.reshape(left_flat.shape[1], -1)
    delta_tile = jnp.dot(left_flat, right_flat, preferred_element_type=jnp.float32)
    return (base_tile.astype(jnp.float32) + delta_tile).astype(jnp.bfloat16)


def body(base_weights, left_factors, right_factors, client_adapter_ranks, step_counts, worker_slot):
    workers = client_adapter_ranks.shape[0]
    rank_cap = right_factors.shape[2]
    rank_slot, slot_scale_factor = slot_tables(client_adapter_ranks, step_counts, worker_slot)
    own_hot = jnp.arange(workers, dtype=jnp.int32) == lax.axis_index("col")
    own_rank = jnp.sum(jnp.where(own_hot, rank_slot, 0))
    own_scale = jnp.sum(jnp.where(own_hot, slot_scale_factor, 0.0))
    rank_scale = jnp.where(jnp.arange(rank_cap, dtype=jnp.int32) < own_rank, own_scale, 0.0)
    scaled_right = (right_factors.astype(jnp.float32) * rank_scale[None, None, :, None]).astype(
        jnp.bfloat16
    )
    merged = [
        merge_tile(base_weights[number], left_factors[number], scaled_right[number])
        for number in range(base_weights.shape[0])
    ]
    return jnp.stack(merged)


def solution(mesh):
    return jax.shard_map(
        body,
        mesh=mesh,
        in_specs=(
            P(None, "row", "col"),
            P(None, "row", "col", None),
            P(None, "col", None, "row"),
            P(),
            P(),
            P(),
        ),
        out_specs=P(None, "row", "col"),
        check_vma=False,
    )
```

profile of v0, /device:TPU:0, one launch (start us, length us, event | category | flops | bytes accessed | tf_op | source)
XLA Modules:
  0.0 342.5 jit_solution(10027888626244682523)
XLA Ops:
  6.5 1.9 fusion.8
  8.4 1.3 convert_reduce_fusion
  9.7 1.3 convert_divide_fusion
  11.0 0.8 select_reduce_fusion.1
  11.8 0.7 select_reduce_fusion
  12.5 0.6 fusion.5
  13.1 0.7 fusion.4
  13.8 2.9 copy.33
  16.7 1.3 compare_select_fusion
  18.1 0.4 multiply_convert_fusion
  18.4 1.0 fusion.7
  19.5 5.2 %all-to-all-start = ((bf16[1,128,8,448]{1,3,0,2:T(8,128)(2,1)}), bf16[1,128,8,448]{1,3,0,2:T(8,128)(2,1)S(1)}, u32[]{:S(2)}, u32[]{:S(2)}) async-start(bf16[1,128,8,448]{1,3,0,2:T(8,128)(2,1)} %bitcast.2), calls=%async_computation | async-start | bytes 1835008 | tf_op jit(solution)/shard_map/all_to_all | solution.py:31
  24.7 0.7 all-gather.15.cloned.1.call-update
  25.4 0.0 all-gather.9.cloned.1.call-start
  25.5 13.2 %all-to-all-done = bf16[1,128,8,448]{1,3,0,2:T(8,128)(2,1)S(1)} async-done(((bf16[1,128,8,448]{1,3,0,2:T(8,128)(2,1)}), bf16[1,128,8,448]{1,3,0,2:T(8,128)(2,1)S(1)}, u32[]{:S(2)}, u32[]{:S(2)}) %all-to-all-start) | async-done | bytes 917536 | tf_op jit(solution)/shard_map/all_to_all | solution.py:31
  38.6 41.8 %all_to_all.40 = bf16[1,128,4,2,448]{1,4,3,0,2:T(8,128)(2,1)} all-to-all(bf16[1,128,4,2,448]{1,4,3,0,2:T(8,128)(2,1)S(1)} %bitcast.63), channel_id=1, replica_groups=mesh['row'=8,'col'=4] {'col'}, dimensions={2} | all-to-all | bytes 1835008 | tf_op jit(solution)/shard_map/all_to_all | solution.py:33
  80.5 0.0 all-gather.13.cloned.1.call-start
  80.6 23.2 %all_to_all.41 = bf16[1,128,8,448]{1,3,0,2:T(8,128)(2,1)S(1)} all-to-all(bf16[1,128,8,448]{1,3,0,2:T(8,128)(2,1)S(1)} %bitcast.60), channel_id=1, replica_groups=mesh['row'=8,'col'=4] {'row'}, dimensions={2} | all-to-all | bytes 1835008 | tf_op jit(solution)/shard_map/all_to_all | solution.py:31
  103.8 25.3 %all_to_all.42 = bf16[1,128,4,2,448]{1,4,3,0,2:T(8,128)(2,1)} all-to-all(bf16[1,128,4,2,448]{1,4,3,0,2:T(8,128)(2,1)S(1)} %bitcast.64), channel_id=1, replica_groups=mesh['row'=8,'col'=4] {'col'}, dimensions={2} | all-to-all | bytes 1835008 | tf_op jit(solution)/shard_map/all_to_all | solution.py:33
  129.1 22.1 %fusion.6 = (bf16[1,1024,7168]{2,1,0:T(8,128)(2,1)}, bf16[1,1024,7168]{2,1,0:T(8,128)(2,1)}) fusion(bf16[2,1024,7168]{2,1,0:T(8,128)(2,1)} %param.6), kind=kLoop, calls=%fused_computation.18 | loop fusion | bytes 58720256 | tf_op jit(solution)/shard_map/slice | solution.py:55
  151.2 19.5 %copy.46 = bf16[1,1024,7168]{1,2,0:T(8,128)(2,1)} copy(bf16[1,1024,7168]{2,1,0:T(8,128)(2,1)} %get-tuple-element.5) | data formatting | bytes 29360128
  170.7 19.9 %copy.47 = bf16[1,1024,7168]{1,2,0:T(8,128)(2,1)} copy(bf16[1,1024,7168]{2,1,0:T(8,128)(2,1)} %get-tuple-element.6) | data formatting | bytes 29360128
  190.6 1.5 copy.38
  192.1 1.5 copy.44
  193.7 18.8 %copy.36 = bf16[4,1,128,1,2,3584]{5,4,2,0,3,1:T(2,128)(2,1)} copy(bf16[4,1,128,1,2,3584]{2,5,4,0,3,1:T(8,128)(2,1)} %all-gather.9.cloned.1.call-done) | data formatting | bytes 14680064 | tf_op jit(solution)/shard_map/all_gather | solution.py:35
  212.4 7.8 %copy.48 = bf16[64,8,2,3584]{3,1,2,0:T(8,128)(2,1)} copy(bf16[64,8,2,3584]{3,2,1,0:T(2,128)(2,1)} %bitcast.56) | data formatting | bytes 14680064
  220.3 18.8 %copy.42 = bf16[4,1,128,1,2,3584]{5,4,2,0,3,1:T(2,128)(2,1)} copy(bf16[4,1,128,1,2,3584]{2,5,4,0,3,1:T(8,128)(2,1)} %all-gather.13.cloned.1.call-done) | data formatting | bytes 14680064 | tf_op jit(solution)/shard_map/all_gather | solution.py:35
  239.0 7.8 %copy.49 = bf16[64,8,2,3584]{3,1,2,0:T(8,128)(2,1)} copy(bf16[64,8,2,3584]{3,2,1,0:T(2,128)(2,1)} %bitcast.57) | data formatting | bytes 14680064
  246.8 16.3 %fusion.2 = bf16[1,1024,7168]{1,2,0:T(8,128)(2,1)} fusion(bf16[512,7168]{1,0:T(8,128)(2,1)} %bitcast.58, bf16[1024,512]{0,1:T(8,128)(2,1)S(1)} %bitcast.65, bf16[1,1024,7168]{1,2,0:T(8,128)(2,1)} %copy.46), kind=kOutput, calls=%fused_computation.5 | convolution fusion | flops 7538212864 | bytes 37748736 | tf_op jit(solution)/shard_map/dot_general | solution.py:39
  263.1 16.5 %fusion.3 = bf16[1,1024,7168]{1,2,0:T(8,128)(2,1)} fusion(bf16[512,7168]{1,0:T(8,128)(2,1)} %bitcast.59, bf16[1024,512]{0,1:T(8,128)(2,1)S(1)} %bitcast.66, bf16[1,1024,7168]{1,2,0:T(8,128)(2,1)} %copy.47), kind=kOutput, calls=%fused_computation.6 | convolution fusion | flops 7538212864 | bytes 37748736 | tf_op jit(solution)/shard_map/dot_general | solution.py:39
  279.6 20.1 %pad_maximum_fusion = bf16[2,1024,7168]{1,2,0:T(8,128)(2,1)} fusion(bf16[1,1024,7168]{1,2,0:T(8,128)(2,1)} %fusion.3, bf16[1,1024,7168]{1,2,0:T(8,128)(2,1)} %fusion.2), kind=kLoop, calls=%fused_computation | loop fusion | flops 14680064 | bytes 58720256 | tf_op jit(solution)/shard_map/stack | solution.py:58
  299.7 36.2 %copy.45 = bf16[2,1024,7168]{2,1,0:T(8,128)(2,1)} copy(bf16[2,1024,7168]{1,2,0:T(8,128)(2,1)} %pad_maximum_fusion) | data formatting | bytes 58720256 | tf_op jit(solution)/shard_map/stack | solution.py:58
  (9 shorter events, 0.1 us)
Async XLA Ops:
  6.5 184.1 %all-gather.11.cloned.1.call-start = ((), (), s32[]{:S(2)}) async-start(), calls=%async_computation.5 | async-start | bytes 1310720 | tf_op jit(solution)/shard_map/all_gather | solution.py:28
  19.5 19.2 %all-to-all-start = ((bf16[1,128,8,448]{1,3,0,2:T(8,128)(2,1)}), bf16[1,128,8,448]{1,3,0,2:T(8,128)(2,1)S(1)}, u32[]{:S(2)}, u32[]{:S(2)}) async-start(bf16[1,128,8,448]{1,3,0,2:T(8,128)(2,1)} %bitcast.2), calls=%async_computation | async-start | bytes 1835008 | tf_op jit(solution)/shard_map/all_to_all | solution.py:31
  24.7 167.5 %all-gather.15.cloned.1.call-start = ((), (), s32[]{:S(2)}) async-start(), calls=%async_computation.7 | async-start | bytes 1310720 | tf_op jit(solution)/shard_map/all_gather | solution.py:28
  25.4 168.2 %all-gather.9.cloned.1.call-start = ((), (), s32[]{:S(2)}) async-start(), calls=%async_computation.4 | async-start | bytes 8257536 | tf_op jit(solution)/shard_map/all_gather | solution.py:35
  80.5 139.8 %all-gather.13.cloned.1.call-start = ((), (), s32[]{:S(2)}) async-start(), calls=%async_computation.6 | async-start | bytes 8257536 | tf_op jit(solution)/shard_map/all_gather | solution.py:35
Sparse Core Ops, SparseCore 0:
  8.9 30.6 all-gather.10
  41.2 39.3 all-gather.14
  82.5 52.3 all-gather.8
  136.7 49.8 all-gather.12
where the time goes:
time: 346 us; the launch traced here: 342 us
  local copies, waits for them, and re-layouts  160 us (46%)
  blocking collectives  90.3 us (26%)
  matrix products  32.8 us (9%)
  other arithmetic  27.2 us (8%)
  waiting for transfers between devices  14 us (4%)
  between operations  13.2 us (4%)
  starting transfers between devices  5.32 us (2%)
    all_to_all x2, blocking collectives, merge_tile(): lax.all_to_all(pair_view, 'col', split_axis=2, concat_axis=0, tiled=True)  67.1 us
    unnamed x5, local copies, waits for them, and re-layouts  57.9 us
    all_gather x2, local copies, waits for them, and re-layouts, merge_tile(): joined = lax.all_gather(join_view, 'row', axis=3, tiled=True)  37.6 us
    another operation x1, local copies, waits for them, and re-layouts, body(): return jnp.stack(merged)  36.2 us
    dot_general x2, matrix products, merge_tile(): jnp.dot(left_flat, right_flat, preferred_element_type=jnp.float32)  32.8 us
    all_to_all x1, blocking collectives, merge_tile(): lax.all_to_all(split_view, 'row', split_axis=2, concat_axis=2, tiled=True)  23.2 us
    slice x1, local copies, waits for them, and re-layouts, body(): base_weights[number]  22.1 us
    another operation x1, other arithmetic, body(): return jnp.stack(merged)  20.1 us
  transfers between devices with their start and end apart: 5, of which 1 were waited for; matrix products, arithmetic and copies ran while one was open for 30% of the time, Pallas kernels for 0%

commit v1 on v0

--- a/solution.py
+++ b/solution.py
@@ -1,9 +1,18 @@
+import functools
 import jax
 import jax.numpy as jnp
 from jax import lax
 from jax.sharding import PartitionSpec as P
 
 ADAPTER_ALPHA = 32
+
+
+def fill_cubes(view, array_axis):
+    w2 = jnp.concatenate(lax.all_gather(view, axis_name="row"), array_axis)
+    return w2
+
+
+press_pipes = functools.partial(fill_cubes, array_axis=3)
 
 
 def slot_tables(client_adapter_ranks, step_counts, worker_slot):
@@ -32,7 +41,7 @@
     pair_view = spread.reshape(1, rank_cap, col_count, row_ratio, sub_width)
     slot_pieces = lax.all_to_all(pair_view, "col", split_axis=2, concat_axis=0, tiled=True)
     join_view = slot_pieces.reshape(col_count, rank_cap, row_ratio, 1, sub_width)
-    joined = lax.all_gather(join_view, "row", axis=3, tiled=True)
+    joined = press_pipes(join_view)
     right_cols = joined.reshape(col_count, rank_cap, row_ratio * block_width)
     left_flat = left_all.reshape(tile_rows, -1)
     right_flat = right_cols.reshape(left_flat.shape[1], -1)

time: 346 us -> 317 us (0.916)
  local copies, waits for them, and re-layouts: 160 us -> 131 us
    unnamed x5 -> x3, local copies, waits for them, and re-layouts: 57.9 us -> 42.4 us
    all_gather x2, local copies, waits for them, and re-layouts: 37.6 us -> 24.6 us  [fill_cubes(): w2 = jnp.concatenate(lax.all_gather(view, axis_name='row'), array_axis)]
  transfers between devices with their start and end apart: 5 -> 5, of which waited for: 1 -> 1; matrix products, arithmetic and copies ran while one was open for 30% -> 28% of each run, Pallas kernels for 0% -> 0%
where the time goes in v1:
time: 317 us; the launch traced here: 314 us
  local copies, waits for them, and re-layouts  131 us (41%)
  blocking collectives  90.3 us (28%)
  matrix products  33.1 us (10%)
  other arithmetic  27.2 us (9%)
  waiting for transfers between devices  14 us (4%)
  between operations  13.2 us (4%)
  starting transfers between devices  5.32 us (2%)
    all_to_all x2, blocking collectives, merge_tile(): lax.all_to_all(pair_view, 'col', split_axis=2, concat_axis=0, tiled=True)  67.1 us
    unnamed x3, local copies, waits for them, and re-layouts  42.4 us
    another operation x1, local copies, waits for them, and re-layouts, body(): return jnp.stack(merged)  36.2 us
    dot_general x2, matrix products, merge_tile(): jnp.dot(left_flat, right_flat, preferred_element_type=jnp.float32)  33.1 us
    all_gather x2, local copies, waits for them, and re-layouts, fill_cubes(): w2 = jnp.concatenate(lax.all_gather(view, axis_name='row'), array_axis)  24.6 us
    all_to_all x1, blocking collectives, merge_tile(): lax.all_to_all(split_view, 'row', split_axis=2, concat_axis=2, tiled=True)  23.2 us
    slice x1, local copies, waits for them, and re-layouts, body(): base_weights[number]  22.1 us
    another operation x1, other arithmetic, body(): return jnp.stack(merged)  20.1 us
  transfers between devices with their start and end apart: 5, of which 1 were waited for; matrix products, arithmetic and copies ran while one was open for 28% of the time, Pallas kernels for 0%

profile of v1, /device:TPU:0, one launch (start us, length us, event | category | flops | bytes accessed | tf_op | source)
XLA Modules:
  0.0 314.4 jit_solution(13219718769815961983)
XLA Ops:
  6.5 1.9 fusion.12
  8.4 1.3 convert_reduce_fusion
  9.7 1.3 convert_divide_fusion
  11.0 0.8 select_reduce_fusion.1
  11.8 0.7 select_reduce_fusion
  12.5 0.6 fusion.9
  13.1 0.7 fusion.8
  13.8 2.9 copy.35
  16.7 1.3 compare_select_fusion
  18.1 0.4 multiply_convert_fusion
  18.4 1.0 fusion.11
  19.5 5.2 %all-to-all-start = ((bf16[1,128,8,448]{1,3,0,2:T(8,128)(2,1)}), bf16[1,128,8,448]{1,3,0,2:T(8,128)(2,1)S(1)}, u32[]{:S(2)}, u32[]{:S(2)}) async-start(bf16[1,128,8,448]{1,3,0,2:T(8,128)(2,1)} %bitcast.2), calls=%async_computation | async-start | bytes 1835008 | tf_op jit(solution)/shard_map/all_to_all | solution.py:40
  24.7 0.0 all-gather.15.cloned.1.call-start
  24.7 0.7 all-gather.15.cloned.1.call-update
  25.4 0.0 all-gather.9.cloned.1.call-start
  25.5 13.2 %all-to-all-done = bf16[1,128,8,448]{1,3,0,2:T(8,128)(2,1)S(1)} async-done(((bf16[1,128,8,448]{1,3,0,2:T(8,128)(2,1)}), bf16[1,128,8,448]{1,3,0,2:T(8,128)(2,1)S(1)}, u32[]{:S(2)}, u32[]{:S(2)}) %all-to-all-start) | async-done | bytes 917536 | tf_op jit(solution)/shard_map/all_to_all | solution.py:40
  38.6 41.8 %all_to_all.40 = bf16[1,128,4,2,448]{1,4,3,0,2:T(8,128)(2,1)} all-to-all(bf16[1,128,4,2,448]{1,4,3,0,2:T(8,128)(2,1)S(1)} %bitcast.75), channel_id=1, replica_groups=mesh['row'=8,'col'=4] {'col'}, dimensions={2} | all-to-all | bytes 1835008 | tf_op jit(solution)/shard_map/all_to_all | solution.py:42
  80.5 0.0 all-gather.13.cloned.1.call-start
  80.6 23.2 %all_to_all.41 = bf16[1,128,8,448]{1,3,0,2:T(8,128)(2,1)S(1)} all-to-all(bf16[1,128,8,448]{1,3,0,2:T(8,128)(2,1)S(1)} %bitcast.72), channel_id=1, replica_groups=mesh['row'=8,'col'=4] {'row'}, dimensions={2} | all-to-all | bytes 1835008 | tf_op jit(solution)/shard_map/all_to_all | solution.py:40
  103.8 25.3 %all_to_all.42 = bf16[1,128,4,2,448]{1,4,3,0,2:T(8,128)(2,1)} all-to-all(bf16[1,128,4,2,448]{1,4,3,0,2:T(8,128)(2,1)S(1)} %bitcast.76), channel_id=1, replica_groups=mesh['row'=8,'col'=4] {'col'}, dimensions={2} | all-to-all | bytes 1835008 | tf_op jit(solution)/shard_map/all_to_all | solution.py:42
  129.1 22.1 %fusion.10 = (bf16[1,1024,7168]{2,1,0:T(8,128)(2,1)}, bf16[1,1024,7168]{2,1,0:T(8,128)(2,1)}) fusion(bf16[2,1024,7168]{2,1,0:T(8,128)(2,1)} %param.6), kind=kLoop, calls=%fused_computation.22 | loop fusion | bytes 58720256 | tf_op jit(solution)/shard_map/slice | solution.py:64
  151.2 19.5 %copy.50 = bf16[1,1024,7168]{1,2,0:T(8,128)(2,1)} copy(bf16[1,1024,7168]{2,1,0:T(8,128)(2,1)} %get-tuple-element.5) | data formatting | bytes 29360128
  170.7 20.0 %copy.51 = bf16[1,1024,7168]{1,2,0:T(8,128)(2,1)} copy(bf16[1,1024,7168]{2,1,0:T(8,128)(2,1)} %get-tuple-element.6) | data formatting | bytes 29360128
  190.7 1.5 copy.41
  192.2 0.0 all-gather.15.cloned.1.call-done
  192.2 1.7 copy.48
  193.9 12.2 %copy.39 = bf16[8,4,128,2,1,448]{2,1,5,0,3,4:T(4,128)(2,1)} copy(bf16[8,4,128,2,1,448]{2,5,3,1,0,4:T(8,128)(2,1)} %bitcast.68) | data formatting | bytes 14680064 | tf_op jit(solution)/shard_map/all_gather | solution.py:11
  206.1 12.5 %copy.46 = bf16[8,4,128,2,1,448]{2,1,5,0,3,4:T(4,128)(2,1)} copy(bf16[8,4,128,2,1,448]{2,5,3,1,0,4:T(8,128)(2,1)} %bitcast.69) | data formatting | bytes 14680064 | tf_op jit(solution)/shard_map/all_gather | solution.py:11
  218.6 16.4 %fusion.2 = bf16[1,1024,7168]{1,2,0:T(8,128)(2,1)} fusion(bf16[1024,512]{0,1:T(8,128)(2,1)S(1)} %bitcast.77, bf16[1,1024,7168]{1,2,0:T(8,128)(2,1)} %copy.50, bf16[896,8,4,128]{3,2,1,0:T(4,128)(2,1)} %bitcast.70), kind=kOutput, calls=%fused_computation.5 | convolution fusion | flops 7538212864 | bytes 37748736 | tf_op jit(solution)/shard_map/dot_general | solution.py:48
  235.0 16.6 %fusion.3 = bf16[1,1024,7168]{1,2,0:T(8,128)(2,1)} fusion(bf16[1024,512]{0,1:T(8,128)(2,1)S(1)} %bitcast.78, bf16[1,1024,7168]{1,2,0:T(8,128)(2,1)} %copy.51, bf16[896,8,4,128]{3,2,1,0:T(4,128)(2,1)} %bitcast.71), kind=kOutput, calls=%fused_computation.6 | convolution fusion | flops 7538212864 | bytes 37748736 | tf_op jit(solution)/shard_map/dot_general | solution.py:48
  251.6 20.1 %pad_maximum_fusion = bf16[2,1024,7168]{1,2,0:T(8,128)(2,1)} fusion(bf16[1,1024,7168]{1,2,0:T(8,128)(2,1)} %fusion.3, bf16[1,1024,7168]{1,2,0:T(8,128)(2,1)} %fusion.2), kind=kLoop, calls=%fused_computation | loop fusion | flops 14680064 | bytes 58720256 | tf_op jit(solution)/shard_map/stack | solution.py:67
  271.7 36.2 %copy.49 = bf16[2,1024,7168]{2,1,0:T(8,128)(2,1)} copy(bf16[2,1024,7168]{1,2,0:T(8,128)(2,1)} %pad_maximum_fusion) | data formatting | bytes 58720256 | tf_op jit(solution)/shard_map/stack | solution.py:67
  (7 shorter events, 0.1 us)
Async XLA Ops:
  6.5 184.2 %all-gather.11.cloned.1.call-start = ((), (), s32[]{:S(2)}) async-start(), calls=%async_computation.5 | async-start | bytes 1310720 | tf_op jit(solution)/shard_map/all_gather | solution.py:37
  19.5 19.2 %all-to-all-start = ((bf16[1,128,8,448]{1,3,0,2:T(8,128)(2,1)}), bf16[1,128,8,448]{1,3,0,2:T(8,128)(2,1)S(1)}, u32[]{:S(2)}, u32[]{:S(2)}) async-start(bf16[1,128,8,448]{1,3,0,2:T(8,128)(2,1)} %bitcast.2), calls=%async_computation | async-start | bytes 1835008 | tf_op jit(solution)/shard_map/all_to_all | solution.py:40
  24.7 167.5 %all-gather.15.cloned.1.call-start = ((), (), s32[]{:S(2)}) async-start(), calls=%async_computation.7 | async-start | bytes 1310720 | tf_op jit(solution)/shard_map/all_gather | solution.py:37
  25.4 168.5 %all-gather.9.cloned.1.call-start = ((), (), s32[]{:S(2)}) async-start(), calls=%async_computation.4 | async-start | bytes 8257536 | tf_op jit(solution)/shard_map/all_gather | solution.py:11
  80.5 125.6 %all-gather.13.cloned.1.call-start = ((), (), s32[]{:S(2)}) async-start(), calls=%async_computation.6 | async-start | bytes 8257536 | tf_op jit(solution)/shard_map/all_gather | solution.py:11
Sparse Core Ops, SparseCore 0:
  8.9 30.6 all-gather.10
  41.2 39.3 all-gather.14
  82.5 52.3 all-gather.8
  136.7 49.8 all-gather.12
